TPU v7x, 32 devices: a whole 2x2x4 slice. The times are simulated.
32 devices in a mesh: sec: 4 (over y, core), dev: 8 (over z, x).
Axes of the slice: x: 2, y: 2, z: 4, core: 2. Of those that a mesh axis runs over, the one named last changes fastest.
Arguments:
- potential: float32 [64, 32, 512], P('dev', None, 'sec'), may hold values from -6 to 6
- previous: float32 [64, 32, 512], P('dev', None, 'sec'), may hold values from -6 to 6
- wave_coeff: float32 [64, 32, 512], P('dev', None, 'sec'), may hold values from 0.03 to 0.16
- sketch_in: bfloat16 [16384, 512], P('dev'), may hold values from -6 to 6
- omega: float32 [64, 512], replicated, may hold values from -6 to 6
- blocks: int32 [8, 9], P('dev'), may hold values from 0 to 255, as said below
- owners: int32 [8, 9], P('dev'), may hold values from 0 to 7, as said below
Outputs:
- basis: bfloat16 [4, 16384, 512], P('sec', 'dev')
- gram_factor: float32 [4, 512, 512], P('sec')
Inputs may be any that keep to these rules, and one draw needn't show every extreme that they name: `blocks`: within one section's 3 entries of a row the block numbers are distinct. Within a row of owners no owner appears more than 2 times, and one owner, the same for all rows, appears exactly 2 times in every row.
All inputs are finite; a program needn't handle non-finite values.
Results may differ from a plain program's by a relative error of at most 0.003.
Values sent between devices are 32-bit elements; how exact they have to be, the bound alone decides.
No kernel may reach another device: no remote copies, remote signals or barrier semaphores. Data moves between devices by JAX's collectives and lax.ppermute only.
A program may use at most 256 MiB of HBM per device.

v0:
```python
import math

import jax
import jax.numpy as jnp
from jax import lax
from jax.sharding import PartitionSpec as P

CAP = 2
STEPS = 16
MB = 4


damping = 0.05
highest = lax.Precision.HIGHEST


def with_halo(x, sides, width):
    for axis, dim in sides:
        size, length = (lax.axis_size(axis), x.shape[dim])
        up = [(i, (i + 1) % size) for i in range(size - 1)]
        down = [(j, i) for i, j in up]
        last = lax.slice_in_dim(x, length - width, length, axis=dim)
        leading = lax.slice_in_dim(x, 0, width, axis=dim)
        before = lax.ppermute(last, axis, up)
        after = lax.ppermute(leading, axis, down)
        x = jnp.concatenate([before, x, after], axis=dim)
    return x


def step_field(current, earlier, stiffness):
    padded = with_halo(current, (("sec", 2), ("dev", 0)), 1)
    padded = jnp.pad(padded, ((0, 0), (1, 1), (0, 0)))
    neighbours = padded[2:, 1:-1, 1:-1] + padded[:-2, 1:-1, 1:-1]
    neighbours = neighbours + padded[1:-1, 2:, 1:-1] + padded[1:-1, :-2, 1:-1]
    neighbours = neighbours + padded[1:-1, 1:-1, 2:] + padded[1:-1, 1:-1, :-2]
    neighbours = neighbours - 6.0 * current
    return 2.0 * current - earlier + stiffness * neighbours - damping * (current - earlier)


def shards(potential, previous, wave_coeff, sketch_in, omega, blocks, owners):
    sections = lax.axis_size("sec")
    column_count = lax.axis_size("dev")
    section = lax.axis_index("sec")
    analysis = section == sections - 1
    keep_mask = jnp.where(analysis, 0.0, 1.0).astype(jnp.float32)
    current = potential * keep_mask
    earlier = previous * keep_mask
    extent_x, extent_y, cells_z = current.shape
    list_width = owners.shape[1]
    per_device = list_width // (sections - 1)
    owner_row = owners[0]
    block_row = blocks[0]
    list_start = jnp.minimum(section, sections - 2) * per_device
    own_cells = lax.dynamic_slice_in_dim(block_row, list_start, per_device)
    position = jnp.arange(list_width, dtype=jnp.int32)
    matches = owner_row[:, None] == owner_row[None, :]
    before = position[:, None] < position[None, :]
    counts = jnp.sum((matches & before).astype(jnp.int32), axis=0)
    slot_index = owner_row * CAP + counts
    ticket_count = column_count * CAP
    placing = (jnp.arange(ticket_count, dtype=jnp.int32)[:, None] == slot_index[None, :]).astype(
        jnp.float32
    )

    def advance(state_pair, unused):
        current, earlier = state_pair
        newest = step_field(current, earlier, wave_coeff) * keep_mask
        snapshot = jnp.take(newest.reshape(extent_x * extent_y, cells_z), own_cells, axis=0)
        return ((newest, current), snapshot)

    sketch_rows = sketch_in.astype(jnp.float32)
    sketch_width = sketch_rows.shape[1]
    for batch_index in range(MB):
        (current, earlier), snapshots = lax.scan(advance, (current, earlier), None, length=STEPS)
        flattened = jnp.transpose(snapshots, (1, 0, 2)).reshape(per_device, STEPS * cells_z)
        placing_own = lax.dynamic_slice_in_dim(placing, list_start, per_device, 1)
        outgoing = jnp.dot(placing_own, flattened, precision=highest).reshape(
            column_count, CAP, STEPS, cells_z
        )
        routed = lax.all_to_all(outgoing, "dev", split_axis=0, concat_axis=0, tiled=True)
        arrived = lax.psum(routed, "sec")
        weights = omega[batch_index * STEPS : (batch_index + 1) * STEPS]
        contribution = jnp.einsum("dcsz,sk->dczk", arrived, weights, precision=highest)
        sketch_rows = sketch_rows + contribution.reshape(-1, sketch_width)
    gram_local = lax.cond(
        analysis,
        lambda: jnp.dot(sketch_rows.T, sketch_rows, precision=highest),
        lambda: jnp.zeros((sketch_width, sketch_width), jnp.float32),
    )
    gram_matrix = lax.psum(gram_local, "dev")
    total_rows = column_count * column_count * CAP * cells_z
    row_scale = math.sqrt(total_rows)

    def finish(gram_total):
        lower_factor = jnp.linalg.cholesky(gram_total)
        basis_rows = (
            jax.scipy.linalg.solve_triangular(lower_factor, sketch_rows.T, lower=True).T * row_scale
        )
        return (basis_rows.astype(jnp.bfloat16), lower_factor.T / row_scale)

    def placeholder(gram_total):
        return (
            jnp.zeros(sketch_rows.shape, jnp.bfloat16),
            jnp.zeros((sketch_width, sketch_width), jnp.float32),
        )

    basis_out, factor = lax.cond(analysis, finish, placeholder, gram_matrix)
    return (basis_out[None], factor[None])


def solution(mesh):
    placed = (
        P("dev", None, "sec"),
        P("dev", None, "sec"),
        P("dev", None, "sec"),
        P("dev", None),
        P(),
        P("dev", None),
        P("dev", None),
    )
    return jax.shard_map(
        shards,
        mesh=mesh,
        in_specs=placed,
        out_specs=(P("sec", "dev", None), P("sec", None, None)),
        check_vma=False,
    )
```

profile of v0, /device:TPU:5, one launch (start us, length us, event | category | flops | bytes accessed | tf_op | source)
XLA Modules:
  0.0 1606.0 jit_solution(16246516462399624769)
XLA Ops:
  10.1 298.7 %while.66 = (s32[]{:T(128)}, f32[8,32,128]{2,1,0:T(8,128)S(1)}, f32[8,32,128]{2,1,0:T(8,128)S(1)}, f32[16,3,128]{2,1,0:T(4,128)S(1)}, f32[8,32,128]{2,1,0:T(8,128)}, /*index=5*/f32[]{:T(128)}, s32[3]{0:T(128)S(1)}, s32[]{:T(128)}) while((s32[]{:T(128)}, f32[8,32,128]{2,1,0:T(8,128)S(1)}, f32[8,32,128]{2,1,0:T(8,128)S(1)}, ...), condition=%wide.region_2.4_spmd, body=%wide.region_1.3_spmd.sunk | while | flops 1302141 | bytes 2013156 | solution.py:74
  25.6 6.9 collective-permute-start.1
  44.1 6.7 collective-permute-start.1
  63.1 6.7 collective-permute-start.1
  82.1 6.7 collective-permute-start.1
  101.1 6.7 collective-permute-start.1
  120.1 6.7 collective-permute-start.1
  139.1 6.7 collective-permute-start.1
  158.1 6.7 collective-permute-start.1
  308.8 304.2 %while.67 = (s32[]{:T(128)}, f32[8,32,128]{2,1,0:T(8,128)S(1)}, f32[8,32,128]{2,1,0:T(8,128)S(1)}, f32[16,3,128]{2,1,0:T(4,128)S(1)}, f32[8,32,128]{2,1,0:T(8,128)}, /*index=5*/f32[]{:T(128)}, s32[3]{0:T(128)S(1)}, s32[]{:T(128)}) while((s32[]{:T(128)}, f32[8,32,128]{2,1,0:T(8,128)S(1)}, f32[8,32,128]{2,1,0:T(8,128)S(1)}, ...), condition=%wide.region_5.7_spmd, body=%wide.region_4.6_spmd.sunk | while | flops 1302141 | bytes 2013156 | solution.py:74
  310.2 6.7 collective-permute-start.5
  329.3 6.7 collective-permute-start.5
  348.3 6.7 collective-permute-start.5
  613.0 304.2 %while.68 = (s32[]{:T(128)}, f32[8,32,128]{2,1,0:T(8,128)S(1)}, f32[8,32,128]{2,1,0:T(8,128)S(1)}, f32[16,3,128]{2,1,0:T(4,128)S(1)}, f32[8,32,128]{2,1,0:T(8,128)}, /*index=5*/f32[]{:T(128)}, s32[3]{0:T(128)S(1)}, s32[]{:T(128)}) while((s32[]{:T(128)}, f32[8,32,128]{2,1,0:T(8,128)S(1)}, f32[8,32,128]{2,1,0:T(8,128)S(1)}, ...), condition=%wide.region_8.10_spmd, body=%wide.region_7.9_spmd.sunk | while | flops 1302141 | bytes 2013156 | solution.py:74
  917.2 304.2 %while.69 = (s32[]{:T(128)}, f32[8,32,128]{2,1,0:T(8,128)S(1)}, f32[8,32,128]{2,1,0:T(8,128)S(1)}, f32[16,3,128]{2,1,0:T(4,128)S(1)}, f32[8,32,128]{2,1,0:T(8,128)}, /*index=5*/f32[]{:T(128)}, s32[3]{0:T(128)S(1)}, s32[]{:T(128)}) while((s32[]{:T(128)}, f32[8,32,128]{2,1,0:T(8,128)S(1)}, f32[8,32,128]{2,1,0:T(8,128)S(1)}, ...), condition=%wide.region_11.13_spmd, body=%wide.region_10.12_spmd.sunk | while | flops 1302141 | bytes 2013156 | solution.py:74
  1222.4 9.9 all-to-all-start.3
  1257.5 9.2 all_to_all.20
  1270.0 35.3 %all-reduce.11.cloned.1.call-done = (f32[8,2,16,128]{3,2,1,0:T(8,128)}, f32[8,2,16,128]{3,2,1,0:T(8,128)}, f32[8,2,16,128]{3,2,1,0:T(8,128)}, f32[8,2,16,128]{3,2,1,0:T(8,128)}) async-done(((f32[8,2,16,128]{3,2,1,0:T(8,128)}, f32[8,2,16,128]{3,2,1,0:T(8,128)}, f32[8,2,16,128]{3,2,1,0:T(8,128)}, f32[8,2,16,128]{3,2,1,0:T(8,128)}), (f32[8,2,16,128]{3,2,1,0:T(8,128)}, f32[8,2,16,128]{3,2,1,0:T(8,128)}, ...) | async-done | bytes 524304 | tf_op jit(solution)/shard_map/psum | solution.py:81
  1348.3 10.3 add_add_fusion
  1358.6 9.7 conditional.2
  1358.8 9.5 fusion.100
  1369.6 78.2 %all-reduce.9.cloned.1.call-done = f32[512,512]{0,1:T(8,128)} async-done(((f32[512,512]{0,1:T(8,128)}), f32[512,512]{0,1:T(8,128)}) %all-reduce.9.cloned.1.call-update) | async-done | bytes 1048592 | tf_op jit(solution)/shard_map/psum | solution.py:90
  1447.8 150.4 %conditional.3 = (bf16[1,2048,512]{2,1,0:T(8,128)(2,1)}, f32[1,512,512]{2,1,0:T(8,128)}) conditional(s32[]{:T(128)} %convert_element_type.30, () %tuple.74, (f32[512,512]{0,1:T(8,128)}, f32[2048,512]{0,1:T(8,128)}) %tuple.80), branch_computations={%region_16.18_spmd, %region_17.27_spmd} | conditional | flops 4439540224 | bytes 64491804 | solution.py:107
  1451.2 11.7 cholesky.5
  1463.0 9.8 custom-call.27
  1473.6 11.7 cholesky.29
  1487.3 9.9 custom-call.28
  1497.9 11.7 cholesky.62
  1511.0 9.8 custom-call.29
  1521.4 11.7 cholesky.89
  1534.7 8.4 while.65
  1543.2 39.3 %custom-call.30 = f32[4,128,128]{1,2,0:T(8,128)S(1)} custom-call(f32[4,128,128]{2,1,0:T(8,128)S(1)} %get-tuple-element.396), custom_call_target="InvertDiagBlocksLowerTriangular" | custom-call | tf_op jit(solution)/shard_map/cond/branch_1_fun/jit(_solve_triangular)/triangular_solve | solution.py:97
  (1309 shorter events, 1238.5 us)
Async XLA Ops:
  24.3 8.3 collective-permute-start
  42.8 8.0 collective-permute-start
  61.8 8.0 collective-permute-start
  80.8 8.0 collective-permute-start
  99.8 8.0 collective-permute-start
  118.8 8.0 collective-permute-start
  137.8 8.0 collective-permute-start
  156.8 8.0 collective-permute-start
  175.8 8.0 collective-permute-start
  308.9 8.0 collective-permute-start.4
  556.1 8.0 collective-permute-start.4
  575.1 8.0 collective-permute-start.4
  594.1 8.0 collective-permute-start.4
  784.2 8.0 collective-permute-start.8
  803.3 8.0 collective-permute-start.8
  822.3 8.0 collective-permute-start.8
  841.3 8.0 collective-permute-start.8
  860.3 8.0 collective-permute-start.8
  879.3 8.0 collective-permute-start.8
  898.3 8.0 collective-permute-start.8
  1012.4 8.0 collective-permute-start.12
  1031.4 8.0 collective-permute-start.12
  1050.4 8.0 collective-permute-start.12
  1069.4 8.0 collective-permute-start.12
  1088.4 8.0 collective-permute-start.12
  1107.4 8.0 collective-permute-start.12
  1126.5 8.0 collective-permute-start.12
  1222.4 16.1 %all-to-all-start.3 = ((f32[8,2,16,128]{3,2,1,0:T(8,128)}), f32[8,2,16,128]{3,2,1,0:T(8,128)S(1)}, u32[]{:S(2)}, u32[]{:S(2)}) async-start(f32[8,2,16,128]{3,2,1,0:T(8,128)} %copy.51), calls=%async_computation.3 | async-start | bytes 262144 | tf_op jit(solution)/shard_map/all_to_all | solution.py:80
  1238.5 9.5 all-to-all-start.2
  1248.0 9.5 all-to-all-start.1
  1251.4 53.9 %all-reduce.11.cloned.1.call-start = ((), (), s32[]{:S(2)}) async-start(), calls=%async_computation.5 | async-start | bytes 1048576 | tf_op jit(solution)/shard_map/psum | solution.py:81
  1266.8 181.0 %all-reduce.9.cloned.1.call-start = ((), (), s32[]{:S(2)}) async-start(), calls=%async_computation.4 | async-start | bytes 2097152 | tf_op jit(solution)/shard_map/psum | solution.py:90
  (239 other events, 1787.4 us)
Sparse Core Ops, SparseCore 0:
  1266.9 38.2 all-reduce.10
  1369.8 77.9 all-reduce.8
where the time goes:
time: 1620 us; the launch traced here: 1610 us
  starting transfers between devices  953 us (59%)
  waiting for transfers between devices  252 us (16%)
  other arithmetic  235 us (15%)
  local copies, waits for them, and re-layouts  85.7 us (5%)
  matrix products  44.6 us (3%)
    ppermute x128, starting transfers between devices, with_halo(): after = lax.ppermute(leading, axis, down)  506 us
    ppermute x128, starting transfers between devices, with_halo(): before = lax.ppermute(last, axis, up)  430 us
    another operation x14, other arithmetic, finish(): lower_factor = jnp.linalg.cholesky(gram_total)  78.5 us
    psum x1, waiting for transfers between devices, shards(): gram_matrix = lax.psum(gram_local, 'dev')  78.2 us
    mul x64, other arithmetic, advance(): newest = step_field(current, earlier, wave_coeff) * keep_mask  78.1 us
    ppermute x128, waiting for transfers between devices, with_halo(): before = lax.ppermute(last, axis, up)  62.9 us
    ppermute x128, waiting for transfers between devices, with_halo(): after = lax.ppermute(leading, axis, down)  59.4 us
    another operation x2, other arithmetic, finish(): jax.scipy.linalg.solve_triangular(lower_factor, sketch_rows.T, lower=True)  39.3 us
  transfers between devices with their start and end apart: 261, of which 133 were waited for; matrix products, arithmetic and copies ran while one was open for 0% of the time, Pallas kernels for 0%

commit v1 on v0

v1 whole, which is shorter than its diff:
```python
import functools
import math

import jax
import jax.numpy as jnp
import numpy as np
from jax import lax
from jax.experimental import pallas as pl
from jax.experimental.pallas import tpu as pltpu
from jax.sharding import PartitionSpec as P

CAP = 2
damping = 0.05
LANES = 128
highest = lax.Precision.HIGHEST
decay = math.sqrt(1.0 - damping)
BOTH = ("sec", "dev")


def neighbour_path(columns):
    order = []
    for i in range(0, columns, 2):
        pair = [i, i + 1]
        order += pair if (i // 2) % 2 == 0 else pair[::-1]
    return order


def vmem(*arrays):
    return [pl.BlockSpec(memory_space=pltpu.VMEM)] * len(arrays)


def big(limit=48):
    return pltpu.CompilerParams(vmem_limit_bytes=limit << 20)


def slab_of(order, column, section, per_slab):
    place = order.index(column)
    forward, backward = place // per_slab, (len(order) - 1 - place) // per_slab
    return jnp.where(section % 2 == 0, forward, backward)


def split_kernel(order, slab, per_slab, u_ref, e_ref, k_ref, table_ref, out_ref, turned):
    section = lax.axis_index("sec")
    extent_x, extent_y, depth = u_ref.shape
    for a, ref in enumerate((u_ref, e_ref, k_ref)):
        for p in range(2):
            rows = jnp.concatenate([ref[x] for x in range(p, extent_x, 2)], axis=0)
            if a == 1:
                rows = rows * decay
            turned[2 * a + p] = rows.T
    for column in range(len(order)):
        at = slab_of(order, column, section, per_slab)
        start = pl.multiple_of(at * slab, 8)
        for q in range(6):
            out_ref[column, q * slab : (q + 1) * slab, :] = turned[q, pl.ds(start, slab), :]
        out_ref[column, 6 * slab :, :] = jnp.broadcast_to(table_ref[...], (8, LANES))


def steps_kernel(
    first_step, slab, per_device, last, snaps, sections,
    table, kl, kc, kr, sl, sc, sr, w_in, *rest,
):
    if last:
        send_ref, w_ref, field_a, field_b, gain, own = rest
    else:
        state_ref, w_ref, field_a, field_b, gain, own = rest
    section = jnp.minimum(lax.axis_index("sec"), sections - 2)
    list_start = section * per_device
    columns = kc.shape[0]
    rows = 3 * slab
    lane = lax.broadcasted_iota(jnp.int32, (8, LANES), 1)
    y_first, y_last = lane % 32 == 0, lane % 32 == 31
    zero = jnp.zeros((8, LANES), jnp.float32)

    for o in range(2 * columns):
        d, p = o // 2, o % 2
        for field, at in ((field_a, p), (field_b, 2 + p)):
            field[o, 0:8, :] = zero
            field[o, 8 + rows : 16 + rows, :] = zero
            for h, ref in enumerate((sl, sc, sr)):
                field[o, 8 + h * slab : 8 + (h + 1) * slab, :] = ref[
                    d, at * slab : (at + 1) * slab, :
                ]
        for h, ref in enumerate((kl, kc, kr)):
            k = ref[d, (4 + p) * slab : (5 + p) * slab, :]
            gain[o, h * slab : (h + 1) * slab, :] = k * (1.0 / decay)
            own[o, h * slab : (h + 1) * slab, :] = ((2.0 - damping) - 6.0 * k) * (1.0 / decay)
    w_ref[...] = w_in[...]

    def step(src, dst, tiles, number):
        for z in tiles:
            at = slice(8 + 8 * z, 16 + 8 * z)
            low = slice(7 + 8 * z, 15 + 8 * z)
            high = slice(9 + 8 * z, 17 + 8 * z)
            here = slice(8 * z, 8 * z + 8)
            values = [src[o, at, :] for o in range(2 * columns)]
            up = [pltpu.roll(values[2 * d + 1], 32, 1) for d in range(columns)]
            down = [pltpu.roll(values[2 * d], LANES - 32, 1) for d in range(columns)]
            for o in range(2 * columns):
                d, p = o // 2, o % 2
                v = values[o]
                if p == 0:
                    side = jnp.where(lane < 32, up[d - 1] if d > 0 else zero, up[d])
                    total = values[o + 1] + side
                else:
                    side = jnp.where(
                        lane >= LANES - 32, down[d + 1] if d + 1 < columns else zero, down[d]
                    )
                    total = values[o - 1] + side
                total = total + (src[o, low, :] + src[o, high, :])
                total = total + jnp.where(y_first, 0.0, pltpu.roll(v, 1, 1))
                total = total + jnp.where(y_last, 0.0, pltpu.roll(v, LANES - 1, 1))
                dst[o, at, :] = own[o, here, :] * v + gain[o, here, :] * total - dst[o, at, :]

        def column_blocks(d, carry):
            for i in range(per_device):
                block = table[d, list_start + i]
                x, y = block >> 5, block & 31
                at_lane = ((x >> 1) << 5) + y
                o = 2 * d + (x & 1)
                j = d * per_device + i
                held = w_ref[j]
                for h in range(slab // 8):
                    target = h * snaps + number
                    value = dst[o, 8 + slab + 8 * h : 16 + slab + 8 * h, :]
                    moved = pltpu.roll(value, (target - at_lane) & (LANES - 1), 1)
                    held = jnp.where(lane == target, moved, held)
                w_ref[j] = held
            return carry

        lax.fori_loop(0, columns, column_blocks, 0, unroll=min(columns, 8))

    for phase in range(slab // 8):
        tiles = range(phase, 3 * slab // 8 - phase)

        def pair(m, carry):
            number = first_step + 8 * phase + 2 * m
            step(field_a, field_b, tiles, number)
            step(field_b, field_a, tiles, number + 1)
            return carry

        lax.fori_loop(0, 4, pair, 0)

    if last:
        send_ref[...] = jnp.zeros(send_ref.shape, jnp.float32)
        width = per_device * (sections - 1)

        def place(d, carry):
            for i in range(per_device):
                mine = table[d, width + list_start + i]

                def earlier(n, c):
                    return c + jnp.where(table[d, width + n] == mine, 1, 0)

                count = lax.fori_loop(0, list_start + i, earlier, 0)
                send_ref[mine, d * CAP + count] = w_ref[d * per_device + i]
            return carry

        lax.fori_loop(0, columns, place, 0)
    else:
        for o in range(2 * columns):
            d, p = o // 2, o % 2
            state_ref[d, p * slab : (p + 1) * slab, :] = field_a[o, 8 + slab : 8 + 2 * slab, :]
            state_ref[d, (2 + p) * slab : (3 + p) * slab, :] = field_b[
                o, 8 + slab : 8 + 2 * slab, :
            ]


def unpack(tile, h, snaps, lane):
    if h:
        tile = pltpu.roll(tile, LANES - h * snaps, 1)
    return jnp.where(lane < snaps, tile, 0.0)


def product_kernel(
    order, slab, per_slab, snaps, sections, w_ref, s_ref, out_ref, sorted_ref, wide, low
):
    section = lax.axis_index("sec")
    slots = w_ref.shape[1]
    halves = slab // 8
    lane = lax.broadcasted_iota(jnp.int32, (8, LANES), 1)
    for column in range(0, len(order)):
        if order.index(column) % per_slab:
            continue
        at = slab_of(order, column, section, per_slab)
        for q in range(slots):
            tile = w_ref[column, q]
            sorted_ref[at, q] = tile
            for h in range(halves):
                w = unpack(tile, h, snaps, lane)
                w1 = w.astype(jnp.bfloat16).astype(jnp.float32)
                w2 = (w - w1).astype(jnp.bfloat16).astype(jnp.float32)
                w3 = w - w1 - w2
                start = pl.multiple_of(q * LANES + at * slab + 8 * h, 8)
                wide[pl.ds(start, 8), :] = w1 + pltpu.roll(w2, snaps, 1)
                low[pl.ds(start, 8), :] = w3
    both = wide[...].astype(jnp.bfloat16)
    tail = low[...].astype(jnp.bfloat16)
    rows = (((0,), (0,)), ((), ()))
    dot = functools.partial(
        lax.dot_general, dimension_numbers=rows, preferred_element_type=jnp.float32
    )
    sketch = s_ref[...]
    a_first = dot(both, sketch)
    a_tail = dot(tail, sketch)
    cross = a_first[:snaps] + (a_first[snaps:] + a_tail[:snaps])
    c_first = dot(both, both)
    c_tail = dot(tail, both)[:snaps, :]
    c_tail = jnp.where(lax.broadcasted_iota(jnp.int32, c_tail.shape, 1) < snaps, c_tail, 0.0)
    half = c_first[:snaps, :] + c_first[snaps:, :]
    own = half + pltpu.roll(half, snaps, 1)
    square = jnp.concatenate([c_tail, jnp.zeros_like(c_tail)], axis=0).T[:snaps, :]
    inner = jnp.where(
        lax.broadcasted_iota(jnp.int32, own.shape, 1) < snaps, own, 0.0
    ) + (c_tail + square)
    keep = jnp.where(section == sections - 1, 0.0, 1.0)
    out_ref[...] = jnp.zeros(out_ref.shape, jnp.float32)
    strips = cross.shape[1] // LANES
    for r in range(snaps // 8):
        for c in range(strips):
            out_ref[r * strips + c, 0] = (
                cross[8 * r : 8 * r + 8, c * LANES : (c + 1) * LANES] * keep
            )
        out_ref[r * strips, 1] = inner[8 * r : 8 * r + 8, :] * keep


def gather_kernel(parts_ref, out_ref):
    total = jnp.sum(parts_ref[...], axis=0)
    for i in range(out_ref.shape[0]):
        out_ref[i] = total


def factor_kernel(scale, sections, parts_ref, omega_ref, s_ref, factor_ref, inverse_ref, g):
    rank = s_ref.shape[0]
    snaps = omega_ref.shape[0]
    strips = rank // LANES
    analysis = lax.axis_index("sec") == sections - 1
    rows_first = (((0,), (0,)), ((), ()))
    cross = jnp.concatenate(
        [
            jnp.concatenate([parts_ref[r * strips + c, 0] for c in range(strips)], axis=1)
            for r in range(snaps // 8)
        ],
        axis=0,
    )
    inner = jnp.concatenate([parts_ref[r * strips, 1] for r in range(snaps // 8)], axis=0)
    omega = omega_ref[...]
    half = cross + 0.5 * jnp.dot(
        inner[:, :snaps], omega, precision=highest, preferred_element_type=jnp.float32
    )
    left = jnp.concatenate([half, omega], axis=0)
    right = jnp.concatenate([omega, half], axis=0)
    g[...] = s_ref[...] + lax.dot_general(
        left, right, rows_first, precision=highest, preferred_element_type=jnp.float32
    )
    row_number = lax.broadcasted_iota(jnp.int32, (rank, rank), 0)
    lane_number = lax.broadcasted_iota(jnp.int32, (rank, rank), 1)
    inverse_ref[...] = jnp.where(row_number == lane_number, 1.0, 0.0)
    sub = lax.broadcasted_iota(jnp.int32, (8, LANES), 0)
    lane = lax.broadcasted_iota(jnp.int32, (8, LANES), 1)
    tiles = LANES // 8

    def block(k, carry):
        start = pl.multiple_of(k * LANES, LANES)
        d = [g[pl.ds(start + 8 * i, 8), pl.ds(start, LANES)] for i in range(tiles)]
        e = [jnp.where(lane == sub + 8 * i, 1.0, 0.0) for i in range(tiles)]
        for j in range(LANES):
            p, r = j // 8, j % 8
            row_d = jnp.broadcast_to(d[p][r : r + 1, :], (8, LANES))
            row_e = jnp.broadcast_to(e[p][r : r + 1, :], (8, LANES))
            inv = 1.0 / jnp.broadcast_to(row_d[:, j : j + 1], (8, LANES))
            row_d = row_d * inv
            row_e = row_e * inv
            for i in range(p, tiles):
                if i == p and r == 7:
                    continue
                col = jnp.broadcast_to(d[i][:, j : j + 1], (8, LANES))
                if i == p:
                    col = jnp.where(sub > r, col, 0.0)
                d[i] = d[i] - col * row_d
                e[i] = e[i] - col * row_e
        own_rows, own_inverse = [], []
        for i in range(tiles):
            diag = lane == sub + 8 * i
            root = lax.rsqrt(jnp.sum(jnp.where(diag, d[i], 0.0), axis=1, keepdims=True))
            own_rows.append(jnp.where(lane >= sub + 8 * i, d[i] * root, 0.0))
            own_inverse.append(e[i] * root)
        upper = jnp.concatenate(own_rows, axis=0)
        small = jnp.concatenate(own_inverse, axis=0)
        panel = jnp.dot(
            small,
            jnp.concatenate([g[pl.ds(start, LANES), :], inverse_ref[pl.ds(start, LANES), :]], 1),
            precision=highest,
            preferred_element_type=jnp.float32,
        )
        lanes_all = lax.broadcasted_iota(jnp.int32, (LANES, rank), 1)
        after = lanes_all >= start + LANES
        fresh = jnp.where(after, panel[:, :rank], 0.0)
        below = panel[:, rank:]
        inverse_ref[pl.ds(start, LANES), :] = below
        change = lax.dot_general(
            fresh,
            jnp.concatenate([fresh, below], axis=1),
            rows_first,
            precision=highest,
            preferred_element_type=jnp.float32,
        )
        factor_ref[pl.ds(start, LANES), :] = fresh
        factor_ref[pl.ds(start, LANES), pl.ds(start, LANES)] = upper
        g[...] = g[...] - change[:, :rank]
        inverse_ref[...] = inverse_ref[...] - change[:, rank:]
        return carry

    lax.fori_loop(0, strips, block, 0)
    factor_ref[...] = jnp.where(analysis, factor_ref[...] * (1.0 / scale), 0.0)
    inverse_ref[...] = inverse_ref[...] * scale


def basis_kernel(
    slab, snaps, sections, inverse_ref, omega_ref, s_ref, w0, w1, w2, out_ref, wide
):
    analysis = lax.axis_index("sec") == sections - 1

    @pl.when(analysis)
    def _():
        lane = lax.broadcasted_iota(jnp.int32, (8, LANES), 1)
        slabs, slots = w0.shape[:2]

        def fill(q, carry):
            for a in range(slabs):
                tile = w0[a, q] + w1[a, q] + w2[a, q]
                for h in range(slab // 8):
                    start = pl.multiple_of(q * LANES + a * slab + 8 * h, 8)
                    wide[pl.ds(start, 8), :] = unpack(tile, h, snaps, lane)
            return carry

        lax.fori_loop(0, slots, fill, 0)
        inverse = inverse_ref[...]
        columns = (((1,), (1,)), ((), ()))
        mixed = lax.dot_general(
            omega_ref[...], inverse, columns, precision=highest, preferred_element_type=jnp.float32
        )
        mixed = jnp.concatenate([mixed, jnp.zeros_like(mixed)], axis=0)
        x1 = inverse.astype(jnp.bfloat16)
        rest = inverse - x1.astype(jnp.float32)
        x2 = rest.astype(jnp.bfloat16)
        rows = 256

        def strip(i, carry):
            at = pl.ds(pl.multiple_of(i * rows, rows), rows)
            s = s_ref[at, :]
            dot = functools.partial(
                lax.dot_general, dimension_numbers=columns, preferred_element_type=jnp.float32
            )
            q = dot(s, x1) + dot(s, x2)
            q = q + jnp.dot(
                wide[at, :], mixed, precision=highest, preferred_element_type=jnp.float32
            )
            out_ref[at, :] = q.astype(jnp.bfloat16)
            return carry

        lax.fori_loop(0, s_ref.shape[0] // rows, strip, 0)

    @pl.when(jnp.logical_not(analysis))
    def _():
        out_ref[...] = jnp.zeros(out_ref.shape, jnp.bfloat16)


def shards(potential, previous, wave_coeff, sketch_in, omega, blocks, owners):
    sections = lax.axis_size("sec")
    columns = lax.axis_size("dev")
    devices = sections * columns
    extent_x, extent_y, depth = potential.shape
    list_width = owners.shape[1]
    per_device = list_width // (sections - 1)
    snaps, rank = omega.shape
    slab = max(8, depth // columns)
    per_slab = slab * columns // depth
    slabs = depth // slab
    slots = columns * CAP
    order = neighbour_path(columns)
    path = []
    for section in range(sections - 1):
        path += [section * columns + d for d in (order if section % 2 == 0 else order[::-1])]
    up = [(path[i], path[i + per_slab]) for i in range(len(path) - per_slab)]
    down = [(b, a) for a, b in up]
    f32 = jnp.float32

    gram = lax.psum(
        lax.dot_general(
            sketch_in, sketch_in, (((0,), (0,)), ((), ())), preferred_element_type=f32
        ),
        "dev",
    )
    scaled = omega * jnp.asarray(
        decay ** np.arange(1, snaps + 1, dtype=np.float64), f32
    )[:, None]

    lists = jnp.pad(
        jnp.concatenate([blocks, owners], axis=1).astype(f32), ((0, 0), (0, LANES - 2 * list_width))
    )
    chunk = 6 * slab + 8
    operands = (potential, previous, wave_coeff, lists)
    outgoing = pl.pallas_call(
        functools.partial(split_kernel, order, slab, per_slab),
        out_shape=jax.ShapeDtypeStruct((columns, chunk, LANES), f32),
        in_specs=vmem(*operands),
        out_specs=pl.BlockSpec(memory_space=pltpu.VMEM),
        scratch_shapes=[pltpu.VMEM((6, depth, LANES), f32)],
        compiler_params=big(),
    )(*operands)
    raw = lax.all_to_all(outgoing, "dev", split_axis=0, concat_axis=0, tiled=True)
    table = raw[:, 6 * slab, : 2 * list_width].astype(jnp.int32)

    def sides(x):
        return lax.ppermute(x, BOTH, up), x, lax.ppermute(x, BOTH, down)

    fields = sides(raw)
    state = fields
    held = jnp.zeros((columns * per_device, 8, LANES), f32)
    rounds = snaps // slab
    for number in range(rounds):
        last = number == rounds - 1
        operands = (table, *fields, *state, held)
        result = (columns, slots, 8, LANES) if last else (columns, 4 * slab, LANES)
        moved, held = pl.pallas_call(
            functools.partial(
                steps_kernel, number * slab, slab, per_device, last, snaps, sections
            ),
            out_shape=(
                jax.ShapeDtypeStruct(result, f32),
                jax.ShapeDtypeStruct(held.shape, f32),
            ),
            in_specs=[pl.BlockSpec(memory_space=pltpu.SMEM)] + vmem(*operands[1:]),
            out_specs=tuple(vmem(0, 0)),
            scratch_shapes=[pltpu.VMEM((2 * columns, 3 * slab + 16, LANES), f32)] * 2
            + [pltpu.VMEM((2 * columns, 3 * slab, LANES), f32)] * 2,
            compiler_params=big(),
        )(*operands)
        if not last:
            state = sides(moved)
    arrived = lax.all_to_all(moved, "dev", split_axis=0, concat_axis=0, tiled=True)

    operands = (arrived, sketch_in)
    parts, ordered = pl.pallas_call(
        functools.partial(product_kernel, order, slab, per_slab, snaps, sections),
        out_shape=(
            jax.ShapeDtypeStruct((devices, 2, 8, LANES), f32),
            jax.ShapeDtypeStruct((slabs, slots, 8, LANES), f32),
        ),
        in_specs=vmem(*operands),
        out_specs=tuple(vmem(0, 0)),
        scratch_shapes=[pltpu.VMEM((slots * depth, LANES), f32)] * 2,
        compiler_params=big(60),
    )(*operands)
    terms = lax.all_to_all(parts, BOTH, split_axis=0, concat_axis=0, tiled=True)
    copies = pl.pallas_call(
        gather_kernel,
        out_shape=jax.ShapeDtypeStruct(terms.shape, f32),
        in_specs=vmem(0),
        out_specs=pl.BlockSpec(memory_space=pltpu.VMEM),
    )(terms)
    sums = lax.all_to_all(copies, BOTH, split_axis=0, concat_axis=0, tiled=True)
    sums, ordered = lax.optimization_barrier((sums, ordered))
    pieces = [lax.ppermute(ordered, "sec", [(i, sections - 1)]) for i in range(sections - 1)]

    scale = math.sqrt(columns * columns * CAP * depth)
    operands = (sums, scaled, gram)
    factor, inverse = pl.pallas_call(
        functools.partial(factor_kernel, scale, sections),
        out_shape=(jax.ShapeDtypeStruct((rank, rank), f32),) * 2,
        in_specs=vmem(*operands),
        out_specs=tuple(vmem(0, 0)),
        scratch_shapes=[pltpu.VMEM((rank, rank), f32)],
        compiler_params=big(),
    )(*operands)
    operands = (inverse, scaled, sketch_in, *pieces)
    basis = pl.pallas_call(
        functools.partial(basis_kernel, slab, snaps, sections),
        out_shape=jax.ShapeDtypeStruct(sketch_in.shape, jnp.bfloat16),
        in_specs=vmem(*operands),
        out_specs=pl.BlockSpec(memory_space=pltpu.VMEM),
        scratch_shapes=[pltpu.VMEM((slots * depth, LANES), f32)],
        compiler_params=big(60),
    )(*operands)
    return (basis[None], factor[None])


def solution(mesh):
    placed = (
        P("dev", None, "sec"),
        P("dev", None, "sec"),
        P("dev", None, "sec"),
        P("dev", None),
        P(),
        P("dev", None),
        P("dev", None),
    )
    return jax.shard_map(
        shards,
        mesh=mesh,
        in_specs=placed,
        out_specs=(P("sec", "dev", None), P("sec", None, None)),
        check_vma=False,
    )
```

time: 1620 us -> 324 us (0.20)
  starting transfers between devices: 953 us -> 57.2 us
  other arithmetic: 235 us -> 0.83 us
  waiting for transfers between devices: 252 us -> 59.9 us
  Pallas kernels: 0 us -> 129 us
  local copies, waits for them, and re-layouts: 85.7 us -> 6.75 us
  blocking collectives: 9.25 us -> 52.5 us
  matrix products: 44.6 us -> 2.25 us
    ppermute x256 -> x11, starting transfers between devices: 936 us -> 9.47 us  [the longest x8 5.43 us: sides(): return (lax.ppermute(x, BOTH, up), x, lax.ppermute(x, BOTH, down))]
    pallas_call x0 -> x9, Pallas kernels: none -> 129 us  [the longest x1 79.8 us: shards(): pl.pallas_call(functools.partial(factor_kernel, scale, sections), out_sha...]
    ppermute x256 -> x11, waiting for transfers between devices: 122 us -> 0.03 us  [the longest x8 0.02 us: sides(): return (lax.ppermute(x, BOTH, up), x, lax.ppermute(x, BOTH, down))]
    another operation x16 -> x0, other arithmetic: 118 us -> none  [the longest x14 78.5 us: finish(): lower_factor = jnp.linalg.cholesky(gram_total)]
    mul x65 -> x1, other arithmetic: 79.1 us -> 0.08 us  [shards(): omega * jnp.asarray(decay ** np.arange(1, snaps + 1, dtype=np.float64), f...]
    psum x2 -> x1, waiting for transfers between devices: 113 us -> 52.5 us  [shards(): lax.psum(lax.dot_general(sketch_in, sketch_in, (((0,), (0,)), ((), ())),...]
    gather x64 -> x0, local copies, waits for them, and re-layouts: 35.8 us -> none  [advance(): jnp.take(newest.reshape(extent_x * extent_y, cells_z), own_cells, axis=0)]
    all_to_all x0 -> x2, blocking collectives: none -> 35.6 us  [the longest x1 19.5 us: shards(): sums = lax.all_to_all(copies, BOTH, split_axis=0, concat_axis=0, tiled=True)]
  transfers between devices with their start and end apart: 261 -> 13, of which waited for: 133 -> 2; matrix products, arithmetic and copies ran while one was open for 0% -> 1% of each run, Pallas kernels for 0% -> 25%
where the time goes in v1:
time: 324 us; the launch traced here: 323 us
  Pallas kernels  129 us (40%)
  waiting for transfers between devices  59.9 us (18%)
  starting transfers between devices  57.2 us (18%)
  blocking collectives  52.5 us (16%)
  between operations  14.3 us (4%)
  local copies, waits for them, and re-layouts  6.75 us (2%)
    pallas_call x1, Pallas kernels, shards(): pl.pallas_call(functools.partial(factor_kernel, scale, sections), out_sha...  79.8 us
    psum x1, waiting for transfers between devices, shards(): lax.psum(lax.dot_general(sketch_in, sketch_in, (((0,), (0,)), ((), ())),...  52.5 us
    all_to_all x1, starting transfers between devices, shards(): terms = lax.all_to_all(parts, BOTH, split_axis=0, concat_axis=0, tiled=True)  47.6 us
    pallas_call x4, Pallas kernels, shards(): pl.pallas_call(functools.partial(steps_kernel, number * slab, slab, per_d...  29.8 us
    all_to_all x1, blocking collectives, shards(): sums = lax.all_to_all(copies, BOTH, split_axis=0, concat_axis=0, tiled=True)  19.5 us
    all_to_all x1, blocking collectives, shards(): lax.all_to_all(outgoing, 'dev', split_axis=0, concat_axis=0, tiled=True)  16.9 us
    all_to_all x1, blocking collectives, shards(): lax.all_to_all(moved, 'dev', split_axis=0, concat_axis=0, tiled=True)  16.1 us
    pallas_call x1, Pallas kernels, shards(): pl.pallas_call(functools.partial(basis_kernel, slab, snaps, sections), ou...  13.2 us
  transfers between devices with their start and end apart: 13, of which 2 were waited for; matrix products, arithmetic and copies ran while one was open for 1% of the time, Pallas kernels for 25%

profile of v1, /device:TPU:5, one launch (start us, length us, event | category | flops | bytes accessed | tf_op | source)
XLA Modules:
  0.0 322.7 jit_solution(14988948820292088726)
XLA Ops:
  7.2 0.7 add_convert_fusion
  7.9 0.9 copy-done.3
  8.8 0.9 copy-done.4
  9.7 0.9 copy-done.5
  10.8 16.9 %all_to_all.20.kc.sc = f32[8,104,128]{2,1,0:T(8,128)S(1)} all-to-all(f32[8,104,128]{2,1,0:T(8,128)S(1)} %shard_map.95), channel_id=1, replica_groups=mesh['sec'=4,'dev'=8] {'dev'}, dimensions={0} | all-to-all | bytes 851968 | tf_op jit(solution)/shard_map/all_to_all | solution.py:412
  28.4 0.7 collective-permute-start
  29.2 6.9 %shard_map.96 = (f32[8,64,128]{2,1,0:T(8,128)S(1)}, f32[24,8,128]{2,1,0:T(8,128)S(1)}) custom-call(s32[8,18]{1,0:T(8,128)S(1)} %bitcast.5, f32[8,104,128]{2,1,0:T(8,128)S(1)} %collective-permute-done.kl.sl, f32[8,104,128]{2,1,0:T(8,128)S(1)} %all_to_all.20.kc.sc, f32[8,104,128]{2,1,0:T(8,128)S(1)} %collective-permute-done.1.kr.sr, ...), custom_call_target="tpu_custom_call" | custom-call | tf_op jit(solution)/shard_map/pallas_call | solution.py:426
  36.0 0.7 collective-permute-start.3
  36.7 0.7 collective-permute-start.2
  37.4 6.9 %shard_map.97 = (f32[8,64,128]{2,1,0:T(8,128)S(1)}, f32[24,8,128]{2,1,0:T(8,128)S(1)}) custom-call(s32[8,18]{1,0:T(8,128)S(1)} %bitcast.6, f32[8,104,128]{2,1,0:T(8,128)S(1)} %collective-permute-done.kl.sl, f32[8,104,128]{2,1,0:T(8,128)S(1)} %all_to_all.20.kc.sc, f32[8,104,128]{2,1,0:T(8,128)S(1)} %collective-permute-done.1.kr.sr, ...), custom_call_target="tpu_custom_call" | custom-call | tf_op jit(solution)/shard_map/pallas_call | solution.py:426
  44.3 0.7 collective-permute-start.5
  45.0 0.7 collective-permute-start.4
  45.7 6.9 %shard_map.98 = (f32[8,64,128]{2,1,0:T(8,128)S(1)}, f32[24,8,128]{2,1,0:T(8,128)S(1)}) custom-call(s32[8,18]{1,0:T(8,128)S(1)} %bitcast.7, f32[8,104,128]{2,1,0:T(8,128)S(1)} %collective-permute-done.kl.sl, f32[8,104,128]{2,1,0:T(8,128)S(1)} %all_to_all.20.kc.sc, f32[8,104,128]{2,1,0:T(8,128)S(1)} %collective-permute-done.1.kr.sr, ...), custom_call_target="tpu_custom_call" | custom-call | tf_op jit(solution)/shard_map/pallas_call | solution.py:426
  53.2 0.7 collective-permute-start.6
  53.9 9.2 %shard_map.99 = (f32[8,16,8,128]{3,2,1,0:T(8,128)S(1)}, f32[24,8,128]{2,1,0:T(8,128)}) custom-call(s32[8,18]{1,0:T(8,128)S(1)} %bitcast.8, f32[8,104,128]{2,1,0:T(8,128)S(1)} %collective-permute-done.kl.sl, f32[8,104,128]{2,1,0:T(8,128)S(1)} %all_to_all.20.kc.sc, f32[8,104,128]{2,1,0:T(8,128)S(1)} %collective-permute-done.1.kr.sr, ...), custom_call_target="tpu_custom_call" | custom-call | tf_op jit(solution)/shard_map/pallas_call | solution.py:426
  63.2 16.1 %all_to_all.21.w_ref = f32[8,16,8,128]{3,2,1,0:T(8,128)} all-to-all(f32[8,16,8,128]{3,2,1,0:T(8,128)S(1)} %get-tuple-element.21), channel_id=1, replica_groups=mesh['sec'=4,'dev'=8] {'dev'}, dimensions={0} | all-to-all | bytes 1048576 | tf_op jit(solution)/shard_map/all_to_all | solution.py:442
  79.3 4.2 %shard_map.100 = (f32[32,2,8,128]{3,2,1,0:T(8,128)}, f32[8,16,8,128]{3,2,1,0:T(8,128)}) custom-call(f32[8,16,8,128]{3,2,1,0:T(8,128)} %all_to_all.21.w_ref, bf16[2048,512]{1,0:T(8,128)(2,1)} %s_ref.3), custom_call_target="tpu_custom_call" | custom-call | tf_op jit(solution)/shard_map/pallas_call | solution.py:445
  83.6 47.6 %all-to-all-start.2 = ((f32[32,2,8,128]{3,2,1,0:T(8,128)}), f32[32,2,8,128]{3,2,1,0:T(8,128)S(1)}, u32[]{:S(2)}, u32[]{:S(2)}) async-start(f32[32,2,8,128]{3,2,1,0:T(8,128)} %get-tuple-element.22), calls=%async_computation.2 | async-start | bytes 524288 | tf_op jit(solution)/shard_map/all_to_all | solution.py:456
  131.3 2.3 fusion
  133.6 7.3 %all-to-all-done.2.parts_ref = f32[32,2,8,128]{3,2,1,0:T(8,128)S(1)} async-done(((f32[32,2,8,128]{3,2,1,0:T(8,128)}), f32[32,2,8,128]{3,2,1,0:T(8,128)S(1)}, u32[]{:S(2)}, u32[]{:S(2)}) %all-to-all-start.2) | async-done | bytes 262176 | tf_op jit(solution)/shard_map/all_to_all | solution.py:456
  140.9 0.7 copy-done.7
  141.6 1.7 shard_map.101
  143.3 19.5 %all_to_all.22.parts_ref = f32[32,2,8,128]{3,2,1,0:T(8,128)S(1)} all-to-all(f32[32,2,8,128]{3,2,1,0:T(8,128)} %shard_map.101), channel_id=1, replica_groups=mesh['sec'=4,'dev'=8] {'sec','dev'}, dimensions={0} | all-to-all | bytes 524288 | tf_op jit(solution)/shard_map/all_to_all | solution.py:463
  162.8 1.3 collective-permute-start.10
  164.1 1.3 collective-permute-start.9
  165.4 1.5 collective-permute-start.8
  167.0 52.5 %all-reduce.3.cloned.1.call-done.s_ref = f32[512,512]{1,0:T(8,128)} async-done(((f32[512,512]{1,0:T(8,128)}), f32[512,512]{1,0:T(8,128)}) %all-reduce.3.cloned.1.call-update) | async-done | bytes 1048592 | tf_op jit(solution)/shard_map/psum | solution.py:389
  219.5 1.2 copy-done.1
  220.7 79.8 %shard_map.102 = (f32[512,512]{1,0:T(8,128)}, f32[512,512]{1,0:T(8,128)S(1)}) custom-call(f32[32,2,8,128]{3,2,1,0:T(8,128)S(1)} %all_to_all.22.parts_ref, f32[64,512]{1,0:T(8,128)S(1)} %broadcast_multiply_fusion.omega_ref, f32[512,512]{1,0:T(8,128)S(1)} %copy-done.1), custom_call_target="tpu_custom_call" | custom-call | tf_op jit(solution)/shard_map/pallas_call | solution.py:469
  300.5 1.0 copy-done.2
  301.6 0.8 copy-done.8
  302.7 13.2 %shard_map.103 = bf16[2048,512]{1,0:T(8,128)(2,1)} custom-call(f32[512,512]{1,0:T(8,128)} %copy-done.2, f32[64,512]{1,0:T(8,128)} %copy-done, bf16[2048,512]{1,0:T(8,128)(2,1)} %s_ref.3, f32[8,16,8,128]{3,2,1,0:T(8,128)} %copy-done.10, f32[8,16,8,128]{3,2,1,0:T(8,128)} %copy-done.9, f32[8,16,8,128]{3,2,1,0:T(8,128)} %copy-done.8), custom_call_target="tpu_custom_call" | custom-call | tf_op jit(solution)/shard_map/pallas_call | solution.py:478
  (41 shorter events, 2.1 us)
Async XLA Ops:
  7.9 0.9 copy-start.3
  8.8 0.9 copy-start.4
  9.7 0.9 copy-start.5
  27.7 1.4 collective-permute-start.1
  28.4 0.7 collective-permute-start
  36.0 1.4 collective-permute-start.3
  36.7 0.7 collective-permute-start.2
  44.3 1.4 collective-permute-start.5
  45.0 0.7 collective-permute-start.4
  52.6 1.4 collective-permute-start.7
  53.2 0.7 collective-permute-start.6
  63.2 68.1 %copy-start.6 = (bf16[2048,512]{1,0:T(8,128)(2,1)S(1)}, bf16[2048,512]{1,0:T(8,128)(2,1)}, u32[]{:S(2)}) copy-start(bf16[2048,512]{1,0:T(8,128)(2,1)} %s_ref.3) | copy-start | bytes 6291460
  83.6 57.3 %all-to-all-start.2 = ((f32[32,2,8,128]{3,2,1,0:T(8,128)}), f32[32,2,8,128]{3,2,1,0:T(8,128)S(1)}, u32[]{:S(2)}, u32[]{:S(2)}) async-start(f32[32,2,8,128]{3,2,1,0:T(8,128)} %get-tuple-element.22), calls=%async_computation.2 | async-start | bytes 524288 | tf_op jit(solution)/shard_map/all_to_all | solution.py:456
  131.2 88.2 %all-reduce.3.cloned.1.call-start = ((), (), s32[]{:S(2)}) async-start(), calls=%async_computation.4 | async-start | bytes 2097152 | tf_op jit(solution)/shard_map/psum | solution.py:389
  133.5 29.2 %copy-start.13 = (f32[8,16,8,128]{3,2,1,0:T(8,128)S(1)}, f32[8,16,8,128]{3,2,1,0:T(8,128)}, u32[]{:S(2)}) copy-start(f32[8,16,8,128]{3,2,1,0:T(8,128)} %get-tuple-element.26) | copy-start | bytes 1572868
  133.6 33.3 %copy-start.11 = (f32[64,512]{1,0:T(8,128)S(1)}, f32[64,512]{1,0:T(8,128)}, u32[]{:S(2)}) copy-start(f32[64,512]{1,0:T(8,128)} %param.12) | copy-start | bytes 393220
  133.6 33.3 %copy-start.12 = (f32[64]{0:T(128)S(1)}, f32[64]{0:T(128)}, u32[]{:S(2)}) copy-start(f32[64]{0:T(128)} %constant.6.clone) | copy-start | bytes 772
  140.9 0.7 copy-start.7
  162.8 138.7 %collective-permute-start.10 = (f32[8,16,8,128]{3,2,1,0:T(8,128)S(1)}, f32[8,16,8,128]{3,2,1,0:T(8,128)S(1)}, u32[]{:S(2)}, u32[]{:S(2)}) collective-permute-start(f32[8,16,8,128]{3,2,1,0:T(8,128)S(1)} %copy-done.13), channel_id=1, source_target_pairs={{16,24},{17,25},{18,26},{19,27},{20,28},{21,29},{22,30},{23,31}} | collective-permute-start | bytes 1572872 | tf_op jit(solution)/shard_map/ppermute | solution.py:465
  164.1 137.5 %collective-permute-start.9 = (f32[8,16,8,128]{3,2,1,0:T(8,128)S(1)}, f32[8,16,8,128]{3,2,1,0:T(8,128)S(1)}, u32[]{:S(2)}, u32[]{:S(2)}) collective-permute-start(f32[8,16,8,128]{3,2,1,0:T(8,128)S(1)} %copy-done.13), channel_id=1, source_target_pairs={{8,24},{9,25},{10,26},{11,27},{12,28},{13,29},{14,30},{15,31}} | collective-permute-start | bytes 1572872 | tf_op jit(solution)/shard_map/ppermute | solution.py:465
  165.4 136.2 %collective-permute-start.8 = (f32[8,16,8,128]{3,2,1,0:T(8,128)S(1)}, f32[8,16,8,128]{3,2,1,0:T(8,128)S(1)}, u32[]{:S(2)}, u32[]{:S(2)}) collective-permute-start(f32[8,16,8,128]{3,2,1,0:T(8,128)S(1)} %copy-done.13), channel_id=1, source_target_pairs={{0,24},{1,25},{2,26},{3,27},{4,28},{5,29},{6,30},{7,31}} | collective-permute-start | bytes 1572872 | tf_op jit(solution)/shard_map/ppermute | solution.py:465
  166.9 134.6 %copy-start = (f32[64,512]{1,0:T(8,128)}, f32[64,512]{1,0:T(8,128)S(1)}, u32[]{:S(2)}) copy-start(f32[64,512]{1,0:T(8,128)S(1)} %broadcast_multiply_fusion.omega_ref) | copy-start | bytes 393220
  219.5 1.2 copy-start.1
  300.5 1.0 copy-start.2
  301.5 0.8 copy-start.8
  301.5 1.0 copy-start.9
  301.5 1.1 copy-start.10
Sparse Core Ops, SparseCore 0:
  136.2 83.2 all-reduce.2

commit v2 on v1

--- a/solution.py
+++ b/solution.py
@@ -230,6 +230,49 @@
         out_ref[i] = total
 
 
+def factor_block(d, e, sub, lane):
+    tiles = len(d)
+    wide = lambda x: jnp.broadcast_to(x, (8, LANES))
+    for p in range(tiles):
+        first = 8 * p
+        cols = [wide(d[p][:, first + j : first + j + 1]) for j in range(8)]
+        s = [[wide(cols[k][j : j + 1, :]) if k >= j else None for k in range(8)] for j in range(8)]
+        t = [wide(d[p][j : j + 1, :]) for j in range(8)]
+        te = [wide(e[p][j : j + 1, :]) for j in range(8)]
+        inv, m = [], [[None] * 8 for _ in range(8)]
+        for j in range(8):
+            inv.append(1.0 / s[j][j])
+            for k in range(j + 1, 8):
+                m[j][k] = s[j][k] * inv[j]
+            for k in range(j + 1, 8):
+                for n in range(k, 8):
+                    s[k][n] = s[k][n] - m[j][k] * s[j][n]
+                t[k] = t[k] - m[j][k] * t[j]
+                te[k] = te[k] - m[j][k] * te[j]
+        if p + 1 < tiles:
+            z, ze = [None] * 8, [None] * 8
+            for j in reversed(range(8)):
+                z[j], ze[j] = t[j] * inv[j], te[j] * inv[j]
+                for k in range(j + 1, 8):
+                    z[j] = z[j] - m[j][k] * z[k]
+                    ze[j] = ze[j] - m[j][k] * ze[k]
+            for i in range(p + 1, tiles):
+                di, ei = d[i], e[i]
+                for j in range(8):
+                    col = wide(d[i][:, first + j : first + j + 1])
+                    di = di - col * z[j]
+                    ei = ei - col * ze[j]
+                d[i], e[i] = di, ei
+        rows, rows_e = t[0] * lax.rsqrt(s[0][0]), te[0] * lax.rsqrt(s[0][0])
+        for j in range(1, 8):
+            root = lax.rsqrt(s[j][j])
+            rows = jnp.where(sub == j, t[j] * root, rows)
+            rows_e = jnp.where(sub == j, te[j] * root, rows_e)
+        d[p] = jnp.where(lane >= sub + first, rows, 0.0)
+        e[p] = rows_e
+    return jnp.concatenate(d, axis=0), jnp.concatenate(e, axis=0)
+
+
 def factor_kernel(scale, sections, parts_ref, omega_ref, s_ref, factor_ref, inverse_ref, g):
     rank = s_ref.shape[0]
     snaps = omega_ref.shape[0]
@@ -264,29 +307,7 @@
         start = pl.multiple_of(k * LANES, LANES)
         d = [g[pl.ds(start + 8 * i, 8), pl.ds(start, LANES)] for i in range(tiles)]
         e = [jnp.where(lane == sub + 8 * i, 1.0, 0.0) for i in range(tiles)]
-        for j in range(LANES):
-            p, r = j // 8, j % 8
-            row_d = jnp.broadcast_to(d[p][r : r + 1, :], (8, LANES))
-            row_e = jnp.broadcast_to(e[p][r : r + 1, :], (8, LANES))
-            inv = 1.0 / jnp.broadcast_to(row_d[:, j : j + 1], (8, LANES))
-            row_d = row_d * inv
-            row_e = row_e * inv
-            for i in range(p, tiles):
-                if i == p and r == 7:
-                    continue
-                col = jnp.broadcast_to(d[i][:, j : j + 1], (8, LANES))
-                if i == p:
-                    col = jnp.where(sub > r, col, 0.0)
-                d[i] = d[i] - col * row_d
-                e[i] = e[i] - col * row_e
-        own_rows, own_inverse = [], []
-        for i in range(tiles):
-            diag = lane == sub + 8 * i
-            root = lax.rsqrt(jnp.sum(jnp.where(diag, d[i], 0.0), axis=1, keepdims=True))
-            own_rows.append(jnp.where(lane >= sub + 8 * i, d[i] * root, 0.0))
-            own_inverse.append(e[i] * root)
-        upper = jnp.concatenate(own_rows, axis=0)
-        small = jnp.concatenate(own_inverse, axis=0)
+        upper, small = factor_block(d, e, sub, lane)
         panel = jnp.dot(
             small,
             jnp.concatenate([g[pl.ds(start, LANES), :], inverse_ref[pl.ds(start, LANES), :]], 1),
@@ -386,11 +407,8 @@
     down = [(b, a) for a, b in up]
     f32 = jnp.float32
 
-    gram = lax.psum(
-        lax.dot_general(
-            sketch_in, sketch_in, (((0,), (0,)), ((), ())), preferred_element_type=f32
-        ),
-        "dev",
+    own_gram = lax.dot_general(
+        sketch_in, sketch_in, (((0,), (0,)), ((), ())), preferred_element_type=f32
     )
     scaled = omega * jnp.asarray(
         decay ** np.arange(1, snaps + 1, dtype=np.float64), f32
@@ -409,6 +427,8 @@
         scratch_shapes=[pltpu.VMEM((6, depth, LANES), f32)],
         compiler_params=big(),
     )(*operands)
+    outgoing, own_gram = lax.optimization_barrier((outgoing, own_gram))
+    gram = lax.psum(own_gram, "dev")
     raw = lax.all_to_all(outgoing, "dev", split_axis=0, concat_axis=0, tiled=True)
     table = raw[:, 6 * slab, : 2 * list_width].astype(jnp.int32)
 

time: 324 us -> 281 us (0.87)
  Pallas kernels: 129 us -> 85.3 us
    pallas_call x1, Pallas kernels: 79.8 us -> 36.1 us  [shards(): pl.pallas_call(functools.partial(factor_kernel, scale, sections), out_sha...]
    unnamed x28 -> x30, local copies, waits for them, and re-layouts: 6.73 us -> 4.04 us
  transfers between devices with their start and end apart: 13 -> 13, of which waited for: 2 -> 2; matrix products, arithmetic and copies ran while one was open for 1% -> 0% of each run, Pallas kernels for 25% -> 13%
where the time goes in v2:
time: 281 us; the launch traced here: 280 us
  Pallas kernels  85.3 us (30%)
  waiting for transfers between devices  62.1 us (22%)
  starting transfers between devices  57.3 us (20%)
  blocking collectives  52.2 us (19%)
  between operations  14.3 us (5%)
  matrix products  4.52 us (2%)
  local copies, waits for them, and re-layouts  4.06 us (1%)
    psum x1, waiting for transfers between devices, shards(): gram = lax.psum(own_gram, 'dev')  52.5 us
    all_to_all x1, starting transfers between devices, shards(): terms = lax.all_to_all(parts, BOTH, split_axis=0, concat_axis=0, tiled=True)  47.8 us
    pallas_call x1, Pallas kernels, shards(): pl.pallas_call(functools.partial(factor_kernel, scale, sections), out_sha...  36.1 us
    pallas_call x4, Pallas kernels, shards(): pl.pallas_call(functools.partial(steps_kernel, number * slab, slab, per_d...  29.8 us
    all_to_all x1, blocking collectives, shards(): sums = lax.all_to_all(copies, BOTH, split_axis=0, concat_axis=0, tiled=True)  19.5 us
    all_to_all x1, blocking collectives, shards(): lax.all_to_all(outgoing, 'dev', split_axis=0, concat_axis=0, tiled=True)  16.9 us
    all_to_all x1, blocking collectives, shards(): lax.all_to_all(moved, 'dev', split_axis=0, concat_axis=0, tiled=True)  15.9 us
    pallas_call x1, Pallas kernels, shards(): pl.pallas_call(functools.partial(basis_kernel, slab, snaps, sections), ou...  13.2 us
  transfers between devices with their start and end apart: 13, of which 2 were waited for; matrix products, arithmetic and copies ran while one was open for 0% of the time, Pallas kernels for 13%

profile of v2, /device:TPU:5, one launch (start us, length us, event | category | flops | bytes accessed | tf_op | source)
XLA Modules:
  0.0 280.1 jit_solution(6551993257664317390)
XLA Ops:
  7.2 4.5 %fusion = f32[512,512]{1,0:T(8,128)} fusion(bf16[2048,512]{1,0:T(8,128)(2,1)} %s_ref.3), kind=kOutput, calls=%fused_computation.3 | convolution fusion | flops 1073741824 | bytes 3145728 | tf_op jit(solution)/shard_map/dot_general | solution.py:410
  11.8 0.2 shard_map.95
  12.1 16.9 %all_to_all.20.kc.sc = f32[8,104,128]{2,1,0:T(8,128)S(1)} all-to-all(f32[8,104,128]{2,1,0:T(8,128)S(1)} %shard_map.95), channel_id=1, replica_groups=mesh['sec'=4,'dev'=8] {'dev'}, dimensions={0} | all-to-all | bytes 851968 | tf_op jit(solution)/shard_map/all_to_all | solution.py:432
  29.0 0.7 collective-permute-start.1
  29.6 0.7 collective-permute-start
  30.4 6.9 %shard_map.96 = (f32[8,64,128]{2,1,0:T(8,128)S(1)}, f32[24,8,128]{2,1,0:T(8,128)S(1)}) custom-call(s32[8,18]{1,0:T(8,128)S(1)} %bitcast.5, f32[8,104,128]{2,1,0:T(8,128)S(1)} %collective-permute-done.kl.sl, f32[8,104,128]{2,1,0:T(8,128)S(1)} %all_to_all.20.kc.sc, f32[8,104,128]{2,1,0:T(8,128)S(1)} %collective-permute-done.1.kr.sr, ...), custom_call_target="tpu_custom_call" | custom-call | tf_op jit(solution)/shard_map/pallas_call | solution.py:446
  37.3 0.7 collective-permute-start.3
  37.9 0.7 collective-permute-start.2
  38.6 6.9 %shard_map.97 = (f32[8,64,128]{2,1,0:T(8,128)S(1)}, f32[24,8,128]{2,1,0:T(8,128)S(1)}) custom-call(s32[8,18]{1,0:T(8,128)S(1)} %bitcast.6, f32[8,104,128]{2,1,0:T(8,128)S(1)} %collective-permute-done.kl.sl, f32[8,104,128]{2,1,0:T(8,128)S(1)} %all_to_all.20.kc.sc, f32[8,104,128]{2,1,0:T(8,128)S(1)} %collective-permute-done.1.kr.sr, ...), custom_call_target="tpu_custom_call" | custom-call | tf_op jit(solution)/shard_map/pallas_call | solution.py:446
  45.5 0.7 collective-permute-start.5
  46.2 0.7 collective-permute-start.4
  46.9 6.9 %shard_map.98 = (f32[8,64,128]{2,1,0:T(8,128)S(1)}, f32[24,8,128]{2,1,0:T(8,128)S(1)}) custom-call(s32[8,18]{1,0:T(8,128)S(1)} %bitcast.7, f32[8,104,128]{2,1,0:T(8,128)S(1)} %collective-permute-done.kl.sl, f32[8,104,128]{2,1,0:T(8,128)S(1)} %all_to_all.20.kc.sc, f32[8,104,128]{2,1,0:T(8,128)S(1)} %collective-permute-done.1.kr.sr, ...), custom_call_target="tpu_custom_call" | custom-call | tf_op jit(solution)/shard_map/pallas_call | solution.py:446
  53.8 0.7 collective-permute-start.7
  54.4 0.7 collective-permute-start.6
  55.2 9.2 %shard_map.99 = (f32[8,16,8,128]{3,2,1,0:T(8,128)S(1)}, f32[24,8,128]{2,1,0:T(8,128)}) custom-call(s32[8,18]{1,0:T(8,128)S(1)} %bitcast.8, f32[8,104,128]{2,1,0:T(8,128)S(1)} %collective-permute-done.kl.sl, f32[8,104,128]{2,1,0:T(8,128)S(1)} %all_to_all.20.kc.sc, f32[8,104,128]{2,1,0:T(8,128)S(1)} %collective-permute-done.1.kr.sr, ...), custom_call_target="tpu_custom_call" | custom-call | tf_op jit(solution)/shard_map/pallas_call | solution.py:446
  64.4 15.9 %all_to_all.21.w_ref = f32[8,16,8,128]{3,2,1,0:T(8,128)} all-to-all(f32[8,16,8,128]{3,2,1,0:T(8,128)S(1)} %get-tuple-element.24), channel_id=1, replica_groups=mesh['sec'=4,'dev'=8] {'dev'}, dimensions={0} | all-to-all | bytes 1048576 | tf_op jit(solution)/shard_map/all_to_all | solution.py:462
  80.3 4.3 %shard_map.100 = (f32[32,2,8,128]{3,2,1,0:T(8,128)}, f32[8,16,8,128]{3,2,1,0:T(8,128)}) custom-call(f32[8,16,8,128]{3,2,1,0:T(8,128)} %all_to_all.21.w_ref, bf16[2048,512]{1,0:T(8,128)(2,1)} %s_ref.3), custom_call_target="tpu_custom_call" | custom-call | tf_op jit(solution)/shard_map/pallas_call | solution.py:465
  84.5 47.8 %all-to-all-start.2 = ((f32[32,2,8,128]{3,2,1,0:T(8,128)}), f32[32,2,8,128]{3,2,1,0:T(8,128)S(1)}, u32[]{:S(2)}, u32[]{:S(2)}) async-start(f32[32,2,8,128]{3,2,1,0:T(8,128)} %get-tuple-element.25), calls=%async_computation.2 | async-start | bytes 524288 | tf_op jit(solution)/shard_map/all_to_all | solution.py:476
  132.4 0.7 all-reduce.3.cloned.1.call-update
  133.1 9.0 %all-to-all-done.2.parts_ref = f32[32,2,8,128]{3,2,1,0:T(8,128)S(1)} async-done(((f32[32,2,8,128]{3,2,1,0:T(8,128)}), f32[32,2,8,128]{3,2,1,0:T(8,128)S(1)}, u32[]{:S(2)}, u32[]{:S(2)}) %all-to-all-start.2) | async-done | bytes 262176 | tf_op jit(solution)/shard_map/all_to_all | solution.py:476
  142.0 0.7 copy-done.6
  142.7 1.7 shard_map.101
  144.4 19.5 %all_to_all.22.parts_ref = f32[32,2,8,128]{3,2,1,0:T(8,128)S(1)} all-to-all(f32[32,2,8,128]{3,2,1,0:T(8,128)} %shard_map.101), channel_id=1, replica_groups=mesh['sec'=4,'dev'=8] {'sec','dev'}, dimensions={0} | all-to-all | bytes 524288 | tf_op jit(solution)/shard_map/all_to_all | solution.py:483
  163.9 1.3 collective-permute-start.10
  165.2 1.3 collective-permute-start.9
  166.5 1.5 collective-permute-start.8
  168.1 52.5 %all-reduce.3.cloned.1.call-done.s_ref = f32[512,512]{1,0:T(8,128)} async-done(((f32[512,512]{1,0:T(8,128)}), f32[512,512]{1,0:T(8,128)}) %all-reduce.3.cloned.1.call-update) | async-done | bytes 1048592 | tf_op jit(solution)/shard_map/psum | solution.py:431
  220.6 1.2 copy-done.1
  221.8 36.1 %shard_map.102 = (f32[512,512]{1,0:T(8,128)}, f32[512,512]{1,0:T(8,128)S(1)}) custom-call(f32[32,2,8,128]{3,2,1,0:T(8,128)S(1)} %all_to_all.22.parts_ref, f32[64,512]{1,0:T(8,128)S(1)} %broadcast_multiply_fusion.omega_ref, f32[512,512]{1,0:T(8,128)S(1)} %copy-done.1), custom_call_target="tpu_custom_call" | custom-call | tf_op jit(solution)/shard_map/pallas_call | solution.py:489
  257.9 1.0 copy-done.2
  258.9 0.8 copy-done.7
  260.0 13.2 %shard_map.103 = bf16[2048,512]{1,0:T(8,128)(2,1)} custom-call(f32[512,512]{1,0:T(8,128)} %copy-done.2, f32[64,512]{1,0:T(8,128)} %copy-done, bf16[2048,512]{1,0:T(8,128)(2,1)} %s_ref.3, f32[8,16,8,128]{3,2,1,0:T(8,128)} %copy-done.9, f32[8,16,8,128]{3,2,1,0:T(8,128)} %copy-done.8, f32[8,16,8,128]{3,2,1,0:T(8,128)} %copy-done.7), custom_call_target="tpu_custom_call" | custom-call | tf_op jit(solution)/shard_map/pallas_call | solution.py:498
  (43 shorter events, 0.6 us)
Async XLA Ops:
  7.2 4.6 %copy-start.13 = (s32[1,9]{1,0:T(1,128)S(1)}, s32[1,9]{1,0:T(1,128)}, u32[]{:S(2)}) copy-start(s32[1,9]{1,0:T(1,128)} %param.14) | copy-start | bytes 112
  7.2 4.6 %copy-start.14 = (s32[1,9]{1,0:T(1,128)S(1)}, s32[1,9]{1,0:T(1,128)}, u32[]{:S(2)}) copy-start(s32[1,9]{1,0:T(1,128)} %param.13) | copy-start | bytes 112
  7.2 4.6 %copy-start.5 = (f32[8,32,128]{2,1,0:T(8,128)S(1)}, f32[8,32,128]{2,1,0:T(8,128)}, u32[]{:S(2)}) copy-start(f32[8,32,128]{2,1,0:T(8,128)} %k_ref.1) | copy-start | bytes 393220
  7.2 4.6 %copy-start.4 = (f32[8,32,128]{2,1,0:T(8,128)S(1)}, f32[8,32,128]{2,1,0:T(8,128)}, u32[]{:S(2)}) copy-start(f32[8,32,128]{2,1,0:T(8,128)} %e_ref.1) | copy-start | bytes 393220
  7.2 4.6 %copy-start.3 = (f32[8,32,128]{2,1,0:T(8,128)S(1)}, f32[8,32,128]{2,1,0:T(8,128)}, u32[]{:S(2)}) copy-start(f32[8,32,128]{2,1,0:T(8,128)} %u_ref.1) | copy-start | bytes 393220
  29.0 1.4 collective-permute-start.1
  29.6 0.7 collective-permute-start
  37.3 1.4 collective-permute-start.3
  37.9 0.7 collective-permute-start.2
  45.5 1.4 collective-permute-start.5
  46.2 0.7 collective-permute-start.4
  53.8 1.4 collective-permute-start.7
  54.4 0.7 collective-permute-start.6
  80.3 87.7 %copy-start.10 = (f32[64,512]{1,0:T(8,128)S(1)}, f32[64,512]{1,0:T(8,128)}, u32[]{:S(2)}) copy-start(f32[64,512]{1,0:T(8,128)} %param.12) | copy-start | bytes 393220
  80.3 87.7 %copy-start.11 = (f32[64]{0:T(128)S(1)}, f32[64]{0:T(128)}, u32[]{:S(2)}) copy-start(f32[64]{0:T(128)} %constant.6.clone) | copy-start | bytes 772
  84.5 79.4 %copy-start.12 = (f32[8,16,8,128]{3,2,1,0:T(8,128)S(1)}, f32[8,16,8,128]{3,2,1,0:T(8,128)}, u32[]{:S(2)}) copy-start(f32[8,16,8,128]{3,2,1,0:T(8,128)} %get-tuple-element.30) | copy-start | bytes 1572868
  84.5 57.5 %all-to-all-start.2 = ((f32[32,2,8,128]{3,2,1,0:T(8,128)}), f32[32,2,8,128]{3,2,1,0:T(8,128)S(1)}, u32[]{:S(2)}, u32[]{:S(2)}) async-start(f32[32,2,8,128]{3,2,1,0:T(8,128)} %get-tuple-element.25), calls=%async_computation.2 | async-start | bytes 524288 | tf_op jit(solution)/shard_map/all_to_all | solution.py:476
  132.3 88.2 %all-reduce.3.cloned.1.call-start = ((), (), s32[]{:S(2)}) async-start(), calls=%async_computation.4 | async-start | bytes 2097152 | tf_op jit(solution)/shard_map/psum | solution.py:431
  142.0 0.7 copy-start.6
  163.9 95.0 %collective-permute-start.10 = (f32[8,16,8,128]{3,2,1,0:T(8,128)S(1)}, f32[8,16,8,128]{3,2,1,0:T(8,128)S(1)}, u32[]{:S(2)}, u32[]{:S(2)}) collective-permute-start(f32[8,16,8,128]{3,2,1,0:T(8,128)S(1)} %copy-done.12), channel_id=1, source_target_pairs={{16,24},{17,25},{18,26},{19,27},{20,28},{21,29},{22,30},{23,31}} | collective-permute-start | bytes 1572872 | tf_op jit(solution)/shard_map/ppermute | solution.py:485
  165.2 93.7 %collective-permute-start.9 = (f32[8,16,8,128]{3,2,1,0:T(8,128)S(1)}, f32[8,16,8,128]{3,2,1,0:T(8,128)S(1)}, u32[]{:S(2)}, u32[]{:S(2)}) collective-permute-start(f32[8,16,8,128]{3,2,1,0:T(8,128)S(1)} %copy-done.12), channel_id=1, source_target_pairs={{8,24},{9,25},{10,26},{11,27},{12,28},{13,29},{14,30},{15,31}} | collective-permute-start | bytes 1572872 | tf_op jit(solution)/shard_map/ppermute | solution.py:485
  166.5 92.4 %collective-permute-start.8 = (f32[8,16,8,128]{3,2,1,0:T(8,128)S(1)}, f32[8,16,8,128]{3,2,1,0:T(8,128)S(1)}, u32[]{:S(2)}, u32[]{:S(2)}) collective-permute-start(f32[8,16,8,128]{3,2,1,0:T(8,128)S(1)} %copy-done.12), channel_id=1, source_target_pairs={{0,24},{1,25},{2,26},{3,27},{4,28},{5,29},{6,30},{7,31}} | collective-permute-start | bytes 1572872 | tf_op jit(solution)/shard_map/ppermute | solution.py:485
  168.1 90.8 %copy-start = (f32[64,512]{1,0:T(8,128)}, f32[64,512]{1,0:T(8,128)S(1)}, u32[]{:S(2)}) copy-start(f32[64,512]{1,0:T(8,128)S(1)} %broadcast_multiply_fusion.omega_ref) | copy-start | bytes 393220
  220.6 1.2 copy-start.1
  257.9 1.0 copy-start.2
  258.9 0.8 copy-start.7
  258.9 1.0 copy-start.8
  258.9 1.1 copy-start.9
Sparse Core Ops, SparseCore 0:
  137.3 83.2 all-reduce.2
